TPU v7x, 32 devices: a whole 2x2x4 slice. The times are simulated.
32 devices in a mesh: clip: 2 (over x), space: 4 (over y, core), tm: 4 (over z).
Axes of the slice: x: 2, y: 2, z: 4, core: 2. Of those that a mesh axis runs over, the one named last changes fastest.
Arguments:
- block_input: bfloat16 [8, 12, 160, 384], P(('clip', 'tm'), 'space'), parts along dimension 0, may hold values from -24 to 24, as said below
- conv_input: bfloat16 [8, 12, 160, 384], P(('clip', 'tm'), 'space'), parts along dimension 0, may hold values from -24 to 24, as said below
- norm_gain: float32 [384], replicated, may hold values from 0.1 to 1.9
- norm_bias: float32 [384], replicated, may hold values from -3 to 3
- conv_weight: bfloat16 [3, 3, 3, 384, 384], replicated, may hold values from -0.0625 to 0.0625
- conv_bias: float32 [384], replicated, may hold values from -1.5 to 1.5
- attn_gain: float32 [384], replicated, may hold values from 0.1 to 1.9
- attn_bias: float32 [384], replicated, may hold values from -1.5 to 1.5
- query_weight: bfloat16 [384, 384], replicated, may hold values from -4 to 4
- query_bias: float32 [384], replicated, may hold values from -1.5 to 1.5
- key_weight: bfloat16 [384, 384], replicated, may hold values from -4 to 4
- value_weight: bfloat16 [384, 384], replicated, may hold values from -0.3125 to 0.3125
- value_bias: float32 [384], replicated, may hold values from -3 to 3
- out_weight: bfloat16 [384, 384], replicated, may hold values from -0.3125 to 0.3125
- out_bias: float32 [384], replicated, may hold values from -3 to 3
Outputs:
- block_output: bfloat16 [8, 12, 160, 384], P(('clip', 'tm'), 'space'), parts along dimension 0
There are 2 independent parts, one for each index of `clip`. A program takes and returns all parts, laid end to end along the dimension named above; an argument that names none is the same for every part. Nothing has to cross between parts.
Inputs may be any that keep to these rules, and one draw needn't show every extreme that they name: `block_input`: finite activations. `conv_input`: finite activations.
All inputs are finite; a program needn't handle non-finite values.
Results may differ from a plain program's by a relative error of at most 0.0075.
Values may be sent and summed in bfloat16 or wider, within the bound.
No kernel may reach another device: no remote copies, remote signals or barrier semaphores. Data moves between devices by JAX's collectives and lax.ppermute only.
A program may use at most 128 MiB of HBM per device.

v0:
```python
import jax
import jax.numpy as jnp
from jax import lax
from jax.sharding import PartitionSpec as P


def from_behind(value, axis, steps):
    count = lax.axis_size(axis)
    leading, last = (max(0, -steps), min(count, count - steps))
    return lax.ppermute(value, axis, [(source, source + steps) for source in range(leading, last)])


def padded_2(x, sides, width):
    for axis, dim in sides:
        peers, length = (lax.axis_size(axis), x.shape[dim])
        up = [(i, (i + 1) % peers) for i in range(peers - 1)]
        down = [(j, i) for i, j in up]
        last = lax.slice_in_dim(x, length - width, length, axis=dim)
        leading = lax.slice_in_dim(x, 0, width, axis=dim)
        before = lax.ppermute(last, axis, up)
        after = lax.ppermute(leading, axis, down)
        x = jnp.concatenate([before, x, after], axis=dim)
    return x


def rms_norm(field, gain, bias):
    mean_square = jnp.mean(field * field, axis=-1, keepdims=True)
    return field * lax.rsqrt(mean_square + 1e-06) * gain + bias


def causal_conv(padded, conv_weight, frame_count, row_count, columns):
    channels = padded.shape[-1]
    running = jnp.zeros((frame_count * row_count * columns, channels), jnp.float32)
    for tap_t in range(3):
        for tap_y in range(3):
            window = padded[tap_t : tap_t + frame_count, tap_y : tap_y + row_count]
            joined = jnp.concatenate(
                [window[:, :, tap_x : tap_x + columns] for tap_x in range(3)], axis=-1
            )
            joined = joined.reshape(-1, 3 * channels)
            kernel = conv_weight[tap_t, tap_y].reshape(3 * channels, channels)
            running = running + jnp.dot(joined, kernel, preferred_element_type=jnp.float32)
    return running.reshape(frame_count, row_count, columns, channels)


def absorb(state, queries, key_rows, value_rows, score_scale):
    numer_acc, denom_acc, max_acc = state
    scores = (
        jnp.einsum("fqc,fkc->fqk", queries, key_rows, preferred_element_type=jnp.float32)
        * score_scale
    )
    new_max = jnp.maximum(max_acc, jnp.max(scores, axis=-1))
    expd = jnp.exp(scores - new_max[..., None])
    weights = expd.astype(jnp.bfloat16)
    added = jnp.einsum("fqk,fkc->fqc", weights, value_rows, preferred_element_type=jnp.float32)
    numer_acc = added
    denom_acc = jnp.sum(expd, axis=-1)
    return (numer_acc, denom_acc, new_max)


def shards(
    block_input,
    conv_input,
    norm_gain,
    norm_bias,
    conv_weight,
    conv_bias,
    attn_gain,
    attn_bias,
    query_weight,
    query_bias,
    key_weight,
    value_weight,
    value_bias,
    out_weight,
    out_bias,
):
    frame_count, row_count, columns, channels = block_input.shape
    field = conv_input.astype(jnp.float32)
    activated = jax.nn.silu(rms_norm(field, norm_gain, norm_bias)).astype(jnp.bfloat16)
    earlier = [from_behind(activated, "tm", offset) for offset in (1, 2)]
    stacked = jnp.concatenate([earlier[1], earlier[0], activated], axis=0)
    padded = padded_2(stacked, (("space", 1),), 1)
    padded = jnp.pad(padded, ((0, 0), (0, 0), (1, 1), (0, 0)))
    convolved = causal_conv(padded, conv_weight, frame_count, row_count, columns) + conv_bias
    mixed = (block_input.astype(jnp.float32) + convolved).astype(jnp.bfloat16)
    mixed_wide = mixed.astype(jnp.float32)
    normed = rms_norm(mixed_wide, attn_gain, attn_bias).astype(jnp.bfloat16)
    flat_rows = normed.reshape(frame_count, row_count * columns, channels)
    score_scale = float(channels) ** (-0.5)
    queries = (
        jnp.dot(flat_rows, query_weight, preferred_element_type=jnp.float32) + query_bias
    ).astype(jnp.bfloat16)
    query_count = row_count * columns
    start_state = (
        jnp.zeros((frame_count, query_count, channels), jnp.float32),
        jnp.zeros((frame_count, query_count), jnp.float32),
        jnp.full((frame_count, query_count), -1e30, jnp.float32),
    )
    source = lax.all_gather(normed, "space", axis=1, tiled=True).reshape(frame_count, -1, channels)
    key_rows = jnp.dot(source, key_weight, preferred_element_type=jnp.float32).astype(jnp.bfloat16)
    value_rows = (
        jnp.dot(source, value_weight, preferred_element_type=jnp.float32) + value_bias
    ).astype(jnp.bfloat16)
    numer_acc, denom_acc, max_acc = absorb(start_state, queries, key_rows, value_rows, score_scale)
    attended = (numer_acc / denom_acc[..., None]).astype(jnp.bfloat16)
    projected = jnp.dot(attended, out_weight, preferred_element_type=jnp.float32) + out_bias
    return (mixed_wide + projected.reshape(mixed_wide.shape)).astype(jnp.bfloat16)


def solution(mesh):
    placed = (
        P(("clip", "tm"), "space", None, None),
        P(("clip", "tm"), "space", None, None),
        P(),
        P(),
        P(),
        P(),
        P(),
        P(),
        P(),
        P(),
        P(),
        P(),
        P(),
        P(),
        P(),
    )
    return jax.shard_map(
        shards,
        mesh=mesh,
        in_specs=placed,
        out_specs=P(("clip", "tm"), "space", None, None),
        check_vma=False,
    )
```

profile of v0, /device:TPU:0, one launch (start us, length us, event | category | flops | bytes accessed | tf_op | source)
XLA Modules:
  0.0 103.6 jit_solution(10755714841860632833)
XLA Ops:
  6.5 1.2 %fusion.35 = f32[3,160]{1,0:T(4,128)S(1)} fusion(bf16[1,3,160,384]{3,2,1,0:T(8,128)(2,1)} %param.16), kind=kLoop, calls=%fused_computation.72 | loop fusion | flops 552480 | bytes 370560 | tf_op jit(solution)/shard_map/reduce_sum | solution.py:27
  7.8 1.3 %fusion.43 = bf16[1,3,160,384]{3,2,1,0:T(8,128)(2,1)S(1)} fusion(bf16[1,3,160,384]{3,2,1,0:T(8,128)(2,1)} %param.16, f32[384]{0:T(512)} %param.18, f32[384]{0:T(512)} %param.17, f32[3,160]{1,0:T(4,128)S(1)} %add_rsqrt_fusion.1), kind=kLoop, calls=%fused_computation.80 | loop fusion | flops 1658880 | bytes 742272 | tf_op jit(solution)/shard_map/convert_element_type | solution.py:80
  9.1 5.0 %collective-permute-start.1 = (bf16[1,3,160,384]{3,2,1,0:T(8,128)(2,1)S(1)}, bf16[1,3,160,384]{3,2,1,0:T(8,128)(2,1)S(1)}, u32[]{:S(2)}, u32[]{:S(2)}) collective-permute-start(bf16[1,3,160,384]{3,2,1,0:T(8,128)(2,1)S(1)} %fusion.43), channel_id=1, source_target_pairs={{0,1},{1,2},{2,3},{4,5},{5,6},{6,7},{8,9},{9,10},{10,11},{12,13},{... | collective-permute-start | bytes 1105928 | tf_op jit(solution)/shard_map/ppermute | solution.py:10
  14.1 4.5 %collective-permute-start = (bf16[1,3,160,384]{3,2,1,0:T(8,128)(2,1)S(1)}, bf16[1,3,160,384]{3,2,1,0:T(8,128)(2,1)S(1)}, u32[]{:S(2)}, u32[]{:S(2)}) collective-permute-start(bf16[1,3,160,384]{3,2,1,0:T(8,128)(2,1)S(1)} %fusion.43), channel_id=1, source_target_pairs={{0,2},{1,3},{4,6},{5,7},{8,10},{9,11},{12,14},{13,15},{16,18},{17,... | collective-permute-start | bytes 1105928 | tf_op jit(solution)/shard_map/ppermute | solution.py:10
  18.6 4.4 %collective-permute-done.1 = bf16[1,3,160,384]{3,2,1,0:T(8,128)(2,1)S(1)} collective-permute-done((bf16[1,3,160,384]{3,2,1,0:T(8,128)(2,1)S(1)}, bf16[1,3,160,384]{3,2,1,0:T(8,128)(2,1)S(1)}, u32[]{:S(2)}, u32[]{:S(2)}) %collective-permute-start.1) | collective-permute-done | bytes 368672 | tf_op jit(solution)/shard_map/ppermute | solution.py:10
  23.0 6.8 %collective-permute-done = bf16[1,3,160,384]{3,2,1,0:T(8,128)(2,1)S(1)} collective-permute-done((bf16[1,3,160,384]{3,2,1,0:T(8,128)(2,1)S(1)}, bf16[1,3,160,384]{3,2,1,0:T(8,128)(2,1)S(1)}, u32[]{:S(2)}, u32[]{:S(2)}) %collective-permute-start) | collective-permute-done | bytes 368672 | tf_op jit(solution)/shard_map/ppermute | solution.py:10
  29.9 1.3 %collective-permute-start.2 = (bf16[3,1,160,384]{3,2,1,0:T(8,128)(2,1)S(1)}, bf16[3,1,160,384]{3,2,1,0:T(8,128)(2,1)S(1)}, u32[]{:S(2)}, u32[]{:S(2)}) collective-permute-start(bf16[3,1,160,384]{3,2,1,0:T(8,128)(2,1)S(1)} %get-tuple-element.41), channel_id=1, source_target_pairs={{0,4},{4,8},{8,12},{1,5},{5,9},{9,13},{2,6},{6,10},{10,14},{3,7},{... | collective-permute-start | bytes 1105928 | tf_op jit(solution)/shard_map/ppermute | solution.py:20
  31.3 1.3 %collective-permute-start.3 = (bf16[3,1,160,384]{3,2,1,0:T(8,128)(2,1)S(1)}, bf16[3,1,160,384]{3,2,1,0:T(8,128)(2,1)S(1)}, u32[]{:S(2)}, u32[]{:S(2)}) collective-permute-start(bf16[3,1,160,384]{3,2,1,0:T(8,128)(2,1)S(1)} %get-tuple-element.40), channel_id=1, source_target_pairs={{4,0},{8,4},{12,8},{5,1},{9,5},{13,9},{6,2},{10,6},{14,10},{7,3},{... | collective-permute-start | bytes 1105928 | tf_op jit(solution)/shard_map/ppermute | solution.py:21
  32.6 3.9 %fusion.53 = (bf16[1,1,3,384,384]{4,3,2,1,0:T(8,128)(2,1)S(1)}, bf16[1,1,3,384,384]{4,3,2,1,0:T(8,128)(2,1)S(1)}, bf16[1,1,3,384,384]{4,3,2,1,0:T(8,128)(2,1)S(1...) fusion(bf16[3,3,3,384,384]{4,3,2,1,0:T(8,128)(2,1)} %param.19), kind=kLoop, calls=%fused_computation.96 | loop fusion | bytes 15925248 | tf_op jit(solution)/shard_map/slice | solution.py:41
  36.6 1.5 %select_maximum_fusion = bf16[3,5,162,384]{3,2,1,0:T(8,128)(2,1)S(1)} fusion(bf16[3,1,160,384]{3,2,1,0:T(8,128)(2,1)S(1)} %collective-permute-done.3, bf16[3,1,160,384]{3,2,1,0:T(8,128)(2,1)S(1)} %collective-permute-done.2, bf16[1,3,160,384]{3,2,1,0:T(8,128)(2,1)S(1)} %fusion.43, bf16[1,3,160,384]{3,2,1,0:T(8,128)(2,1)S(1)} %collective-permute-done.1, ...), kind=kLoop, calls=%fused_computation.10 | loop fusion | flops 16796160 | bytes 3709440 | tf_op jit(solution)/shard_map/concatenate | solution.py:22
  38.1 1.1 %fusion.54 = (bf16[1,3,160,384]{3,2,1,0:T(8,128)(2,1)S(1)}, bf16[1,3,160,384]{3,2,1,0:T(8,128)(2,1)S(1)}, bf16[1,3,160,384]{3,2,1,0:T(8,128)(2,1)S(1)}, bf16[1,3...) fusion(bf16[3,5,162,384]{3,2,1,0:T(8,128)(2,1)S(1)} %select_max, ...), kind=kLoop, calls=%fused_computation.97 | loop fusion | bytes 13271040 | tf_op jit(solution)/shard_map/slice | solution.py:38
  39.3 1.3 %fusion.26 = (bf16[1,3,160,1152]{3,2,1,0:T(8,128)(2,1)S(1)}, bf16[1,3,160,1152]{3,2,1,0:T(8,128)(2,1)S(1)}, bf16[1,3,160,1152]{3,2,1,0:T(8,128)(2,1)S(1)}) fusion(bf16[3,1,160,384]{3,2,1,0:T(8,128)(2,1)S(1)} %collective-permute-done.2, bf16[1,3,160,384]{3,2,1,0:T(8,128)(2,1)S(1)} %fusion.43, bf16[1,3,160,384]{3,2,1,0:T(8,128)(2,1)S(1)} %collective-permute-done.1, ...), kind=kLoop, calls=%fused_computation.41 | loop fusion | flops 19906560 | bytes 7004160 | tf_op jit(solution)/shard_map/concatenate | solution.py:37
  40.5 0.8 fusion.55
  41.4 0.2 pad_maximum_fusion.18
  41.6 0.8 convolution_add_fusion.10
  42.4 0.5 fusion.24
  43.0 0.8 convolution_add_fusion.9
  43.7 0.8 convolution_add_fusion.8
  44.5 0.8 convolution_add_fusion.7
  45.3 0.8 convolution_add_fusion.6
  46.0 0.8 convolution_add_fusion.5
  46.8 0.8 convolution_add_fusion.4
  47.6 0.8 convolution_add_fusion.3
  48.8 0.9 fusion.47
  49.8 1.4 %fusion.14 = bf16[480,384]{1,0:T(8,128)(2,1)S(1)} fusion(bf16[480,384]{1,0:T(8,128)(2,1)} %bitcast.75, bf16[384,384]{1,0:T(8,128)(2,1)S(1)} %copy-done.7, f32[384]{0:T(512)S(1)} %copy-done.10), kind=kOutput, calls=%fused_computation.31 | convolution fusion | flops 141926400 | bytes 1033728 | tf_op jit(solution)/shard_map/dot_general | solution.py:92
  51.2 32.2 %all-gather.2.cloned.1.call-done = bf16[1,12,160,384]{3,2,0,1:T(8,128)(2,1)} async-done(((bf16[1,3,160,384]{3,2,0,1:T(8,128)(2,1)}), bf16[1,12,160,384]{3,2,0,1:T(8,128)(2,1)}) %all-gather.2.cloned.1.call-update) | async-done | bytes 1474576 | tf_op jit(solution)/shard_map/all_gather | solution.py:100
  83.4 5.3 %multiply_reduce_fusion = (f32[480]{0:T(512)S(1)}, f32[480,1920]{1,0:T(8,128)}) fusion(bf16[480,384]{1,0:T(8,128)(2,1)S(1)} %fusion.14, bf16[1920,384]{1,0:T(8,128)(2,1)} %bitcast.79, bf16[384,384]{1,0:T(8,128)(2,1)S(1)} %copy-done), kind=kOutput, calls=%fused_computation.4 | convolution fusion | flops 1276599808 | bytes 5826432 | tf_op jit(solution)/shard_map/fqc,fkc->fqk/dot_general | solution.py:49
  88.7 2.2 %fusion.3 = bf16[1920,384]{1,0:T(8,128)(2,1)} fusion(bf16[1920,384]{1,0:T(8,128)(2,1)S(1)} %bitcast.80, bf16[384,384]{1,0:T(8,128)(2,1)S(1)} %copy-done.8, f32[384]{0:T(512)S(1)} %copy-done.11), kind=kOutput, calls=%fused_computation.9 | convolution fusion | flops 567705600 | bytes 3245568 | tf_op jit(solution)/shard_map/dot_general | solution.py:103
  90.9 0.7 fusion.1
  91.9 0.5 copy-done.13
  92.4 3.5 %convolution_add_fusion.1 = f32[480,384]{1,0:T(8,128)S(1)} fusion(bf16[384,384]{1,0:T(8,128)(2,1)S(1)} %copy-done.9, bf16[1920,384]{1,0:T(8,128)(2,1)S(1)} %copy-done.13, f32[480,1920]{1,0:T(8,128)} %get-tuple-element.43, f32[480]{0:T(512)S(1)} %broadcast_maximum_fusion, f32[384]{0:T(512)S(1)} %copy-done.12, f32[480]{0:T(512)S(1)} %fusion.1), kind=kOutput, calls=%fused_computation.21 | convolution fusion | flops 852664320 | bytes 6198528 | tf_op jit(solution)/shard_map/dot_general | solution.py:107
  96.0 0.8 fusion.49
  (37 shorter events, 0.9 us)
Async XLA Ops:
  6.5 76.8 %copy-start = (bf16[384,384]{1,0:T(8,128)(2,1)S(1)}, bf16[384,384]{1,0:T(8,128)(2,1)}, u32[]{:S(2)}) copy-start(bf16[384,384]{1,0:T(8,128)(2,1)} %param.25) | copy-start | bytes 884740
  6.5 76.8 %all-gather.2.cloned.1.call-start = ((), (), s32[]{:S(2)}) async-start(), calls=%async_computation | async-start | bytes 1843200 | tf_op jit(solution)/shard_map/all_gather | solution.py:100
  9.1 13.9 %collective-permute-start.1 = (bf16[1,3,160,384]{3,2,1,0:T(8,128)(2,1)S(1)}, bf16[1,3,160,384]{3,2,1,0:T(8,128)(2,1)S(1)}, u32[]{:S(2)}, u32[]{:S(2)}) collective-permute-start(bf16[1,3,160,384]{3,2,1,0:T(8,128)(2,1)S(1)} %fusion.43), channel_id=1, source_target_pairs={{0,1},{1,2},{2,3},{4,5},{5,6},{6,7},{8,9},{9,10},{10,11},{12,13},{... | collective-permute-start | bytes 1105928 | tf_op jit(solution)/shard_map/ppermute | solution.py:10
  14.1 15.8 %collective-permute-start = (bf16[1,3,160,384]{3,2,1,0:T(8,128)(2,1)S(1)}, bf16[1,3,160,384]{3,2,1,0:T(8,128)(2,1)S(1)}, u32[]{:S(2)}, u32[]{:S(2)}) collective-permute-start(bf16[1,3,160,384]{3,2,1,0:T(8,128)(2,1)S(1)} %fusion.43), channel_id=1, source_target_pairs={{0,2},{1,3},{4,6},{5,7},{8,10},{9,11},{12,14},{13,15},{16,18},{17,... | collective-permute-start | bytes 1105928 | tf_op jit(solution)/shard_map/ppermute | solution.py:10
  29.9 6.6 %collective-permute-start.2 = (bf16[3,1,160,384]{3,2,1,0:T(8,128)(2,1)S(1)}, bf16[3,1,160,384]{3,2,1,0:T(8,128)(2,1)S(1)}, u32[]{:S(2)}, u32[]{:S(2)}) collective-permute-start(bf16[3,1,160,384]{3,2,1,0:T(8,128)(2,1)S(1)} %get-tuple-element.41), channel_id=1, source_target_pairs={{0,4},{4,8},{8,12},{1,5},{5,9},{9,13},{2,6},{6,10},{10,14},{3,7},{... | collective-permute-start | bytes 1105928 | tf_op jit(solution)/shard_map/ppermute | solution.py:20
  31.3 5.3 %collective-permute-start.3 = (bf16[3,1,160,384]{3,2,1,0:T(8,128)(2,1)S(1)}, bf16[3,1,160,384]{3,2,1,0:T(8,128)(2,1)S(1)}, u32[]{:S(2)}, u32[]{:S(2)}) collective-permute-start(bf16[3,1,160,384]{3,2,1,0:T(8,128)(2,1)S(1)} %get-tuple-element.40), channel_id=1, source_target_pairs={{4,0},{8,4},{12,8},{5,1},{9,5},{13,9},{6,2},{10,6},{14,10},{7,3},{... | collective-permute-start | bytes 1105928 | tf_op jit(solution)/shard_map/ppermute | solution.py:21
  47.6 1.0 copy-start.2
  47.6 1.0 copy-start.3
  47.6 1.2 %copy-start.4 = (f32[384]{0:T(512)S(1)}, f32[384]{0:T(512)}, u32[]{:S(2)}) copy-start(f32[384]{0:T(512)} %param.22) | copy-start | bytes 4612
  47.6 1.2 %copy-start.5 = (f32[384]{0:T(512)S(1)}, f32[384]{0:T(512)}, u32[]{:S(2)}) copy-start(f32[384]{0:T(512)} %param.21) | copy-start | bytes 4612
  48.4 1.4 %copy-start.7 = (bf16[384,384]{1,0:T(8,128)(2,1)S(1)}, bf16[384,384]{1,0:T(8,128)(2,1)}, u32[]{:S(2)}) copy-start(bf16[384,384]{1,0:T(8,128)(2,1)} %param.23) | copy-start | bytes 884740
  48.4 1.4 %copy-start.10 = (f32[384]{0:T(512)S(1)}, f32[384]{0:T(512)}, u32[]{:S(2)}) copy-start(f32[384]{0:T(512)} %param.24) | copy-start | bytes 4612
  83.3 5.4 %copy-start.6 = (bf16[1,12,160,384]{3,2,0,1:T(8,128)(2,1)S(1)}, bf16[1,12,160,384]{3,2,0,1:T(8,128)(2,1)}, u32[]{:S(2)}) copy-start(bf16[1,12,160,384]{3,2,0,1:T(8,128)(2,1)} %all-gather.2.cloned.1.call-done) | copy-start | bytes 4423684
  83.3 5.4 %copy-start.8 = (bf16[384,384]{1,0:T(8,128)(2,1)S(1)}, bf16[384,384]{1,0:T(8,128)(2,1)}, u32[]{:S(2)}) copy-start(bf16[384,384]{1,0:T(8,128)(2,1)} %param.26) | copy-start | bytes 884740
  83.3 5.4 %copy-start.11 = (f32[384]{0:T(512)S(1)}, f32[384]{0:T(512)}, u32[]{:S(2)}) copy-start(f32[384]{0:T(512)} %param.27) | copy-start | bytes 4612
  88.7 2.2 %copy-start.1 = (f32[480,1920]{1,0:T(8,128)S(1)}, f32[480,1920]{1,0:T(8,128)}, u32[]{:S(2)}) copy-start(f32[480,1920]{1,0:T(8,128)} %get-tuple-element.43) | copy-start | bytes 11059204
  90.9 1.0 copy-start.9
  90.9 1.0 copy-start.12
  90.9 1.5 %copy-start.13 = (bf16[1920,384]{1,0:T(8,128)(2,1)S(1)}, bf16[1920,384]{1,0:T(8,128)(2,1)}, u32[]{:S(2)}) copy-start(bf16[1920,384]{1,0:T(8,128)(2,1)} %fusion.3) | copy-start | bytes 4423684
Sparse Core Ops, SparseCore 0:
  49.9 33.4 all-gather.1
where the time goes:
time: 104 us
  waiting for transfers between devices  43.5 us (42%)
  matrix products  19.3 us (19%)
  between operations  13.7 us (13%)
  starting transfers between devices  12.1 us (12%)
  other arithmetic  9.02 us (9%)
  local copies, waits for them, and re-layouts  6.02 us (6%)
    all_gather x1, waiting for transfers between devices, shards(): lax.all_gather(normed, 'space', axis=1, tiled=True)  32.2 us
    ppermute x2, waiting for transfers between devices, from_behind(): lax.ppermute(value, axis, [(source, source + steps) for source in range(l...  11.2 us
    ppermute x2, starting transfers between devices, from_behind(): lax.ppermute(value, axis, [(source, source + steps) for source in range(l...  9.48 us
    dot_general x9, matrix products, causal_conv(): jnp.dot(joined, kernel, preferred_element_type=jnp.float32)  6.87 us
    dot_general x1, matrix products, absorb(): jnp.einsum('fqc,fkc->fqk', queries, key_rows, preferred_element_type=jnp....  5.34 us
    slice x1, local copies, waits for them, and re-layouts, causal_conv(): kernel = conv_weight[tap_t, tap_y].reshape(3 * channels, channels)  3.94 us
    dot_general x1, matrix products, shards(): jnp.dot(attended, out_weight, preferred_element_type=jnp.float32) + out_bias  3.54 us
    dot_general x1, matrix products, shards(): jnp.dot(source, value_weight, preferred_element_type=jnp.float32)  2.19 us
  transfers between devices with their start and end apart: 5, of which 4 were waited for; matrix products, arithmetic and copies ran while one was open for 5% of the time, Pallas kernels for 0%

commit v1 on v0

--- a/solution.py
+++ b/solution.py
@@ -2,6 +2,24 @@
 import jax.numpy as jnp
 from jax import lax
 from jax.sharding import PartitionSpec as P
+
+
+def gather_around(value, axis, dim):
+    ways, here, step = (lax.axis_size(axis), lax.axis_index(axis), value.shape[dim])
+    lengths = [n * ways if d == dim else n for d, n in enumerate(value.shape)]
+    full = lax.dynamic_update_slice_in_dim(
+        jnp.zeros(lengths, value.dtype), value, here * step, axis=dim
+    )
+    going_up = going_down = value
+    for far in range(1, ways // 2 + 1):
+        going_up = lax.ppermute(going_up, axis, [(d, (d + 1) % ways) for d in range(ways)])
+        full = lax.dynamic_update_slice_in_dim(full, going_up, (here - far) % ways * step, axis=dim)
+        if 2 * far < ways:
+            going_down = lax.ppermute(going_down, axis, [(d, (d - 1) % ways) for d in range(ways)])
+            full = lax.dynamic_update_slice_in_dim(
+                full, going_down, (here + far) % ways * step, axis=dim
+            )
+    return full
 
 
 def from_behind(value, axis, steps):
@@ -97,7 +115,7 @@
         jnp.zeros((frame_count, query_count), jnp.float32),
         jnp.full((frame_count, query_count), -1e30, jnp.float32),
     )
-    source = lax.all_gather(normed, "space", axis=1, tiled=True).reshape(frame_count, -1, channels)
+    source = gather_around(normed, "space", 1).reshape(frame_count, -1, channels)
     key_rows = jnp.dot(source, key_weight, preferred_element_type=jnp.float32).astype(jnp.bfloat16)
     value_rows = (
         jnp.dot(source, value_weight, preferred_element_type=jnp.float32) + value_bias

time: 104 us -> 84.6 us (0.81)
  the two profiles are of different devices: /device:TPU:0 before, /device:TPU:20 now
where the time goes in v1:
time: 84.6 us; the launch traced here: 84.4 us
  waiting for transfers between devices  40 us (47%)
  matrix products  15.7 us (19%)
  starting transfers between devices  12.4 us (15%)
  other arithmetic  10.2 us (12%)
  local copies, waits for them, and re-layouts  5.76 us (7%)
    ppermute x2, waiting for transfers between devices, from_behind(): lax.ppermute(value, axis, [(source, source + steps) for source in range(l...  24.2 us
    ppermute x2, waiting for transfers between devices, gather_around(): lax.ppermute(going_up, axis, [(d, (d + 1) % ways) for d in range(ways)])  14.7 us
    dot_general x9, matrix products, causal_conv(): jnp.dot(joined, kernel, preferred_element_type=jnp.float32)  6.85 us
    ppermute x2, starting transfers between devices, from_behind(): lax.ppermute(value, axis, [(source, source + steps) for source in range(l...  4.78 us
    dot_general x1, matrix products, absorb(): jnp.einsum('fqk,fkc->fqc', weights, value_rows, preferred_element_type=jn...  4.16 us
    slice x1, local copies, waits for them, and re-layouts, causal_conv(): kernel = conv_weight[tap_t, tap_y].reshape(3 * channels, channels)  3.92 us
    dot_general x1, matrix products, absorb(): jnp.einsum('fqc,fkc->fqk', queries, key_rows, preferred_element_type=jnp....  3.89 us
    ppermute x1, starting transfers between devices, padded_2(): after = lax.ppermute(leading, axis, down)  3.64 us
  transfers between devices with their start and end apart: 7, of which 5 were waited for; matrix products, arithmetic and copies ran while one was open for 5% of the time, Pallas kernels for 0%

profile of v1, /device:TPU:20, one launch (start us, length us, event | category | flops | bytes accessed | tf_op | source)
XLA Modules:
  0.0 84.4 jit_solution(10213105879706401952)
XLA Ops:
  0.0 1.2 %fusion.33 = f32[3,160]{1,0:T(4,128)S(1)} fusion(bf16[1,3,160,384]{3,2,1,0:T(8,128)(2,1)} %param.16), kind=kLoop, calls=%fused_computation.72 | loop fusion | flops 552480 | bytes 370560 | tf_op jit(solution)/shard_map/reduce_sum | solution.py:45
  1.2 1.3 %fusion.41 = bf16[1,3,160,384]{3,2,1,0:T(8,128)(2,1)S(1)} fusion(bf16[1,3,160,384]{3,2,1,0:T(8,128)(2,1)} %param.16, f32[384]{0:T(512)} %param.18, f32[384]{0:T(512)} %param.17, f32[3,160]{1,0:T(4,128)S(1)} %add_rsqrt_fusion.1), kind=kLoop, calls=%fused_computation.80 | loop fusion | flops 1658880 | bytes 742272 | tf_op jit(solution)/shard_map/convert_element_type | solution.py:98
  2.6 1.3 %collective-permute-start = (bf16[1,3,160,384]{3,2,1,0:T(8,128)(2,1)S(1)}, bf16[1,3,160,384]{3,2,1,0:T(8,128)(2,1)S(1)}, u32[]{:S(2)}, u32[]{:S(2)}) collective-permute-start(bf16[1,3,160,384]{3,2,1,0:T(8,128)(2,1)S(1)} %fusion.41), channel_id=1, source_target_pairs={{0,2},{1,3},{4,6},{5,7},{8,10},{9,11},{12,14},{13,15},{16,18},{17,... | collective-permute-start | bytes 1105928 | tf_op jit(solution)/shard_map/ppermute | solution.py:28
  3.9 3.5 %collective-permute-start.1 = (bf16[1,3,160,384]{3,2,1,0:T(8,128)(2,1)S(1)}, bf16[1,3,160,384]{3,2,1,0:T(8,128)(2,1)S(1)}, u32[]{:S(2)}, u32[]{:S(2)}) collective-permute-start(bf16[1,3,160,384]{3,2,1,0:T(8,128)(2,1)S(1)} %fusion.41), channel_id=1, source_target_pairs={{0,1},{1,2},{2,3},{4,5},{5,6},{6,7},{8,9},{9,10},{10,11},{12,13},{... | collective-permute-start | bytes 1105928 | tf_op jit(solution)/shard_map/ppermute | solution.py:28
  7.4 9.5 %collective-permute-done = bf16[1,3,160,384]{3,2,1,0:T(8,128)(2,1)S(1)} collective-permute-done((bf16[1,3,160,384]{3,2,1,0:T(8,128)(2,1)S(1)}, bf16[1,3,160,384]{3,2,1,0:T(8,128)(2,1)S(1)}, u32[]{:S(2)}, u32[]{:S(2)}) %collective-permute-start) | collective-permute-done | bytes 368672 | tf_op jit(solution)/shard_map/ppermute | solution.py:28
  16.9 14.7 %collective-permute-done.1 = bf16[1,3,160,384]{3,2,1,0:T(8,128)(2,1)S(1)} collective-permute-done((bf16[1,3,160,384]{3,2,1,0:T(8,128)(2,1)S(1)}, bf16[1,3,160,384]{3,2,1,0:T(8,128)(2,1)S(1)}, u32[]{:S(2)}, u32[]{:S(2)}) %collective-permute-start.1) | collective-permute-done | bytes 368672 | tf_op jit(solution)/shard_map/ppermute | solution.py:28
  31.6 1.9 %collective-permute-start.2 = (bf16[3,1,160,384]{3,2,1,0:T(8,128)(2,1)S(1)}, bf16[3,1,160,384]{3,2,1,0:T(8,128)(2,1)S(1)}, u32[]{:S(2)}, u32[]{:S(2)}) collective-permute-start(bf16[3,1,160,384]{3,2,1,0:T(8,128)(2,1)S(1)} %get-tuple-element.43), channel_id=1, source_target_pairs={{0,4},{4,8},{8,12},{1,5},{5,9},{9,13},{2,6},{6,10},{10,14},{3,7},{... | collective-permute-start | bytes 1105928 | tf_op jit(solution)/shard_map/ppermute | solution.py:38
  33.6 3.6 %collective-permute-start.3 = (bf16[3,1,160,384]{3,2,1,0:T(8,128)(2,1)S(1)}, bf16[3,1,160,384]{3,2,1,0:T(8,128)(2,1)S(1)}, u32[]{:S(2)}, u32[]{:S(2)}) collective-permute-start(bf16[3,1,160,384]{3,2,1,0:T(8,128)(2,1)S(1)} %get-tuple-element.42), channel_id=1, source_target_pairs={{4,0},{8,4},{12,8},{5,1},{9,5},{13,9},{6,2},{10,6},{14,10},{7,3},{... | collective-permute-start | bytes 1105928 | tf_op jit(solution)/shard_map/ppermute | solution.py:39
  37.2 3.9 %fusion.49 = (bf16[1,1,3,384,384]{4,3,2,1,0:T(8,128)(2,1)S(1)}, bf16[1,1,3,384,384]{4,3,2,1,0:T(8,128)(2,1)S(1)}, bf16[1,1,3,384,384]{4,3,2,1,0:T(8,128)(2,1)S(1...) fusion(bf16[3,3,3,384,384]{4,3,2,1,0:T(8,128)(2,1)} %param.19), kind=kLoop, calls=%fused_computation.98 | loop fusion | bytes 15925248 | tf_op jit(solution)/shard_map/slice | solution.py:59
  41.1 1.1 %collective-permute-done.3 = bf16[3,1,160,384]{3,2,1,0:T(8,128)(2,1)S(1)} collective-permute-done((bf16[3,1,160,384]{3,2,1,0:T(8,128)(2,1)S(1)}, bf16[3,1,160,384]{3,2,1,0:T(8,128)(2,1)S(1)}, u32[]{:S(2)}, u32[]{:S(2)}) %collective-permute-start.3) | collective-permute-done | bytes 368672 | tf_op jit(solution)/shard_map/ppermute | solution.py:39
  42.2 1.5 %select_maximum_fusion = bf16[3,5,162,384]{3,2,1,0:T(8,128)(2,1)S(1)} fusion(bf16[3,1,160,384]{3,2,1,0:T(8,128)(2,1)S(1)} %collective-permute-done.3, bf16[3,1,160,384]{3,2,1,0:T(8,128)(2,1)S(1)} %collective-permute-done.2, bf16[1,3,160,384]{3,2,1,0:T(8,128)(2,1)S(1)} %fusion.41, bf16[1,3,160,384]{3,2,1,0:T(8,128)(2,1)S(1)} %collective-permute-done.1, ...), kind=kLoop, calls=%fused_computation.10 | loop fusion | flops 16796160 | bytes 3709440 | tf_op jit(solution)/shard_map/concatenate | solution.py:40
  43.8 1.1 %fusion.50 = (bf16[1,3,160,384]{3,2,1,0:T(8,128)(2,1)S(1)}, bf16[1,3,160,384]{3,2,1,0:T(8,128)(2,1)S(1)}, bf16[1,3,160,384]{3,2,1,0:T(8,128)(2,1)S(1)}, bf16[1,3...) fusion(bf16[3,5,162,384]{3,2,1,0:T(8,128)(2,1)S(1)} %select_max, ...), kind=kLoop, calls=%fused_computation.99 | loop fusion | bytes 13271040 | tf_op jit(solution)/shard_map/slice | solution.py:56
  44.9 1.3 %fusion.18 = (bf16[1,3,160,1152]{3,2,1,0:T(8,128)(2,1)S(1)}, bf16[1,3,160,1152]{3,2,1,0:T(8,128)(2,1)S(1)}, bf16[1,3,160,1152]{3,2,1,0:T(8,128)(2,1)S(1)}) fusion(bf16[3,1,160,384]{3,2,1,0:T(8,128)(2,1)S(1)} %collective-permute-done.2, bf16[1,3,160,384]{3,2,1,0:T(8,128)(2,1)S(1)} %fusion.41, bf16[1,3,160,384]{3,2,1,0:T(8,128)(2,1)S(1)} %collective-permute-done.1, ...), kind=kLoop, calls=%fused_computation.39 | loop fusion | flops 19906560 | bytes 7004160 | tf_op jit(solution)/shard_map/concatenate | solution.py:55
  46.2 0.8 fusion.51
  47.3 0.8 convolution_add_fusion.10
  48.1 0.4 fusion.16
  48.4 0.8 convolution_add_fusion.9
  49.2 0.8 convolution_add_fusion.8
  50.0 0.8 convolution_add_fusion.7
  50.7 0.8 convolution_add_fusion.6
  51.5 0.8 convolution_add_fusion.5
  52.3 0.8 convolution_add_fusion.4
  53.1 0.8 convolution_add_fusion.3
  54.9 2.0 %collective-permute-start.5 = (bf16[1,3,160,384]{3,2,1,0:T(8,128)(2,1)S(1)}, bf16[1,3,160,384]{3,2,1,0:T(8,128)(2,1)S(1)}, u32[]{:S(2)}, u32[]{:S(2)}) collective-permute-start(bf16[1,3,160,384]{3,2,1,0:T(8,128)(2,1)S(1)} %get-tuple-element.6), channel_id=1, source_target_pairs={{0,12},{4,0},{8,4},{12,8},{1,13},{5,1},{9,5},{13,9},{2,14},{6,2},{... | collective-permute-start | bytes 1105928 | tf_op jit(solution)/shard_map/ppermute | solution.py:18
  56.9 8.3 %collective-permute-done.4 = bf16[1,3,160,384]{3,2,1,0:T(8,128)(2,1)S(1)} collective-permute-done((bf16[1,3,160,384]{3,2,1,0:T(8,128)(2,1)S(1)}, bf16[1,3,160,384]{3,2,1,0:T(8,128)(2,1)S(1)}, u32[]{:S(2)}, u32[]{:S(2)}) %collective-permute-start.4) | collective-permute-done | bytes 368672 | tf_op jit(solution)/shard_map/ppermute | solution.py:15
  65.2 0.4 fusion.14
  65.8 6.4 %collective-permute-done.6 = bf16[1,3,160,384]{3,2,1,0:T(8,128)(2,1)S(1)} collective-permute-done((bf16[1,3,160,384]{3,2,1,0:T(8,128)(2,1)S(1)}, bf16[1,3,160,384]{3,2,1,0:T(8,128)(2,1)S(1)}, u32[]{:S(2)}, u32[]{:S(2)}) %collective-permute-start.6) | collective-permute-done | bytes 368672 | tf_op jit(solution)/shard_map/ppermute | solution.py:15
  72.2 3.9 %multiply_reduce_fusion = (f32[480]{0:T(512)S(1)}, f32[480,1920]{1,0:T(8,128)}) fusion(bf16[480,384]{1,0:T(8,128)(2,1)S(1)} %fusion.14, bf16[1920,384]{1,0:T(8,128)(2,1)S(1)} %bitcast.67, bf16[384,384]{1,0:T(8,128)(2,1)S(1)} %copy-done), kind=kOutput, calls=%fused_computation.4 | convolution fusion | flops 1276599808 | bytes 5826432 | tf_op jit(solution)/shard_map/fqc,fkc->fqk/dot_general | solution.py:67
  76.1 2.8 %fusion.1 = f32[480]{0:T(512)S(1)} fusion(f32[480,1920]{1,0:T(8,128)} %get-tuple-element.45, f32[480]{0:T(512)S(1)} %broadcast_maximum_fusion), kind=kLoop, calls=%fused_computation.5 | loop fusion | flops 2764320 | bytes 3690240 | tf_op jit(solution)/shard_map/reduce_sum | solution.py:75
  79.0 4.2 %fusion.30 = bf16[480,384]{1,0:T(8,128)(2,1)S(1)} fusion(bf16[1920,384]{1,0:T(8,128)(2,1)S(1)} %bitcast.68, bf16[384,384]{1,0:T(8,128)(2,1)S(1)} %copy-done.8, f32[384]{0:T(512)S(1)} %copy-done.10, f32[480,1920]{1,0:T(8,128)} %get-tuple-element.45, f32[480]{0:T(512)S(1)} %broadcast_maximum_fusion, f32[480]{0:T(512)S(1)} %fusion.1), kind=kOutput, calls=%fused_computation.69 | convolution fusion | flops 1278627840 | bytes 5829888 | tf_op jit(solution)/shard_map/fqk,fkc->fqc/dot_general | solution.py:73
  83.2 0.4 convolution_add_fusion.1
  83.6 0.8 fusion.46
  (38 shorter events, 1.7 us)
Async XLA Ops:
  0.0 72.2 %copy-start = (bf16[384,384]{1,0:T(8,128)(2,1)S(1)}, bf16[384,384]{1,0:T(8,128)(2,1)}, u32[]{:S(2)}) copy-start(bf16[384,384]{1,0:T(8,128)(2,1)} %param.25) | copy-start | bytes 884740
  2.6 14.3 %collective-permute-start = (bf16[1,3,160,384]{3,2,1,0:T(8,128)(2,1)S(1)}, bf16[1,3,160,384]{3,2,1,0:T(8,128)(2,1)S(1)}, u32[]{:S(2)}, u32[]{:S(2)}) collective-permute-start(bf16[1,3,160,384]{3,2,1,0:T(8,128)(2,1)S(1)} %fusion.41), channel_id=1, source_target_pairs={{0,2},{1,3},{4,6},{5,7},{8,10},{9,11},{12,14},{13,15},{16,18},{17,... | collective-permute-start | bytes 1105928 | tf_op jit(solution)/shard_map/ppermute | solution.py:28
  3.9 27.7 %collective-permute-start.1 = (bf16[1,3,160,384]{3,2,1,0:T(8,128)(2,1)S(1)}, bf16[1,3,160,384]{3,2,1,0:T(8,128)(2,1)S(1)}, u32[]{:S(2)}, u32[]{:S(2)}) collective-permute-start(bf16[1,3,160,384]{3,2,1,0:T(8,128)(2,1)S(1)} %fusion.41), channel_id=1, source_target_pairs={{0,1},{1,2},{2,3},{4,5},{5,6},{6,7},{8,9},{9,10},{10,11},{12,13},{... | collective-permute-start | bytes 1105928 | tf_op jit(solution)/shard_map/ppermute | solution.py:28
  31.6 9.5 %collective-permute-start.2 = (bf16[3,1,160,384]{3,2,1,0:T(8,128)(2,1)S(1)}, bf16[3,1,160,384]{3,2,1,0:T(8,128)(2,1)S(1)}, u32[]{:S(2)}, u32[]{:S(2)}) collective-permute-start(bf16[3,1,160,384]{3,2,1,0:T(8,128)(2,1)S(1)} %get-tuple-element.43), channel_id=1, source_target_pairs={{0,4},{4,8},{8,12},{1,5},{5,9},{9,13},{2,6},{6,10},{10,14},{3,7},{... | collective-permute-start | bytes 1105928 | tf_op jit(solution)/shard_map/ppermute | solution.py:38
  33.6 8.7 %collective-permute-start.3 = (bf16[3,1,160,384]{3,2,1,0:T(8,128)(2,1)S(1)}, bf16[3,1,160,384]{3,2,1,0:T(8,128)(2,1)S(1)}, u32[]{:S(2)}, u32[]{:S(2)}) collective-permute-start(bf16[3,1,160,384]{3,2,1,0:T(8,128)(2,1)S(1)} %get-tuple-element.42), channel_id=1, source_target_pairs={{4,0},{8,4},{12,8},{5,1},{9,5},{13,9},{6,2},{10,6},{14,10},{7,3},{... | collective-permute-start | bytes 1105928 | tf_op jit(solution)/shard_map/ppermute | solution.py:39
  53.1 1.0 %copy-start.1 = (bf16[1,3,160,384]{3,2,1,0:T(8,128)(2,1)S(1)}, bf16[1,3,160,384]{3,2,1,0:T(8,128)(2,1)}, u32[]{:S(2)}) copy-start(bf16[1,3,160,384]{3,2,1,0:T(8,128)(2,1)} %param.15) | copy-start | bytes 1105924
  53.1 1.0 %copy-start.3 = (f32[384]{0:T(512)S(1)}, f32[384]{0:T(512)}, u32[]{:S(2)}) copy-start(f32[384]{0:T(512)} %param.20) | copy-start | bytes 4612
  53.9 0.7 copy-start.4
  53.9 0.7 copy-start.5
  54.0 11.2 %copy-start.7 = (bf16[384,384]{1,0:T(8,128)(2,1)S(1)}, bf16[384,384]{1,0:T(8,128)(2,1)}, u32[]{:S(2)}) copy-start(bf16[384,384]{1,0:T(8,128)(2,1)} %param.23) | copy-start | bytes 884740
  54.0 11.2 %copy-start.9 = (f32[384]{0:T(512)S(1)}, f32[384]{0:T(512)}, u32[]{:S(2)}) copy-start(f32[384]{0:T(512)} %param.24) | copy-start | bytes 4612
  54.8 10.4 %collective-permute-start.4 = (bf16[1,3,160,384]{3,2,1,0:T(8,128)(2,1)S(1)}, bf16[1,3,160,384]{3,2,1,0:T(8,128)(2,1)S(1)}, u32[]{:S(2)}, u32[]{:S(2)}) collective-permute-start(bf16[1,3,160,384]{3,2,1,0:T(8,128)(2,1)S(1)} %get-tuple-element.6), channel_id=1, source_target_pairs={{0,4},{4,8},{8,12},{12,0},{1,5},{5,9},{9,13},{13,1},{2,6},{6,10},{... | collective-permute-start | bytes 1105928 | tf_op jit(solution)/shard_map/ppermute | solution.py:15
  54.9 10.8 %collective-permute-start.5 = (bf16[1,3,160,384]{3,2,1,0:T(8,128)(2,1)S(1)}, bf16[1,3,160,384]{3,2,1,0:T(8,128)(2,1)S(1)}, u32[]{:S(2)}, u32[]{:S(2)}) collective-permute-start(bf16[1,3,160,384]{3,2,1,0:T(8,128)(2,1)S(1)} %get-tuple-element.6), channel_id=1, source_target_pairs={{0,12},{4,0},{8,4},{12,8},{1,13},{5,1},{9,5},{13,9},{2,14},{6,2},{... | collective-permute-start | bytes 1105928 | tf_op jit(solution)/shard_map/ppermute | solution.py:18
  65.2 6.9 %collective-permute-start.6 = (bf16[1,3,160,384]{3,2,1,0:T(8,128)(2,1)S(1)}, bf16[1,3,160,384]{3,2,1,0:T(8,128)(2,1)S(1)}, u32[]{:S(2)}, u32[]{:S(2)}) collective-permute-start(bf16[1,3,160,384]{3,2,1,0:T(8,128)(2,1)S(1)} %collective-permute-done.4), channel_id=1, source_target_pairs={{0,4},{4,8},{8,12},{12,0},{1,5},{5,9},{9,13},{13,1},{2,6},{6,10},{... | collective-permute-start | bytes 1105928 | tf_op jit(solution)/shard_map/ppermute | solution.py:15
  76.1 2.8 %copy-start.8 = (bf16[384,384]{1,0:T(8,128)(2,1)S(1)}, bf16[384,384]{1,0:T(8,128)(2,1)}, u32[]{:S(2)}) copy-start(bf16[384,384]{1,0:T(8,128)(2,1)} %param.26) | copy-start | bytes 884740
  76.1 2.8 %copy-start.10 = (f32[384]{0:T(512)S(1)}, f32[384]{0:T(512)}, u32[]{:S(2)}) copy-start(f32[384]{0:T(512)} %param.27) | copy-start | bytes 4612
  79.0 4.2 %copy-start.2 = (bf16[384,384]{1,0:T(8,128)(2,1)S(1)}, bf16[384,384]{1,0:T(8,128)(2,1)}, u32[]{:S(2)}) copy-start(bf16[384,384]{1,0:T(8,128)(2,1)} %param.28) | copy-start | bytes 884740
  79.0 4.2 %copy-start.6 = (f32[384]{0:T(512)S(1)}, f32[384]{0:T(512)}, u32[]{:S(2)}) copy-start(f32[384]{0:T(512)} %param.29) | copy-start | bytes 4612
